TPU v7x, 512 devices: a whole 4x4x16 slice. The times are simulated.
512 devices in a mesh: dp: 8 (over y, z_hi), tensor: 64 (over x, z_lo, core).
Axes of the slice: x: 4, y: 4, z: 16 (z_hi: 2, z_lo: 8; z = z_hi * 8 + z_lo), core: 2. Of those that a mesh axis runs over, the one named last changes fastest.
Arguments:
- tokens: bfloat16 [8192, 8192], P('dp', 'tensor'), may hold values from -6 to 6
- first_up: bfloat16 [64, 128, 128], P('tensor'), may hold values from -0.5 to 0.5
- second_up: bfloat16 [128, 64, 256], P('tensor'), may hold values from -0.75 to 0.75
- first_down: bfloat16 [128, 256, 64], P('tensor'), may hold values from -0.375 to 0.375
- second_down: bfloat16 [64, 128, 128], P('tensor'), may hold values from -0.5 to 0.5
- out_grad: bfloat16 [8192, 8192], P('dp', 'tensor'), may hold values from -6 to 6
Outputs:
- output: bfloat16 [8192, 8192], P('dp', 'tensor')
- tokens_grad: bfloat16 [8192, 8192], P('dp', 'tensor')
- first_up_grad: float32 [64, 128, 128], P('tensor')
- second_up_grad: float32 [128, 64, 256], P('tensor')
- first_down_grad: float32 [128, 256, 64], P('tensor')
- second_down_grad: float32 [64, 128, 128], P('tensor')
All inputs are finite; a program needn't handle non-finite values.
Results may differ from a plain program's by a relative error of at most 0.0095.
Values may be sent and summed in bfloat16 or wider, within the bound.
A program may use at most 64 MiB of HBM per device.

v0:
```python
import math
import jax
import jax.numpy as jnp
from jax import lax
from jax.sharding import PartitionSpec as P


def cdf_part(value):
    return 0.5 * (1.0 + jax.scipy.special.erf(value / math.sqrt(2.0)))


def gelu_deriv(value):
    return cdf_part(value) + value * jnp.exp(-0.5 * value * value) / math.sqrt(2.0 * math.pi)


def middle_work(upper_cols, second_up, first_down):
    f32 = jnp.float32
    bf16 = jnp.bfloat16
    pre = jnp.einsum("jbt,jbo->jot", upper_cols, second_up, preferred_element_type=f32).astype(bf16)
    prefl = pre.astype(f32)
    act = (prefl * cdf_part(prefl)).astype(bf16)
    zeta = jnp.einsum("jot,job->jbt", act, first_down, preferred_element_type=f32).astype(bf16)
    return (pre, act, zeta)


def column_backward(dzeta_cols, act, pre, upper_cols, second_up, first_down):
    f32 = jnp.float32
    bf16 = jnp.bfloat16
    grad_d1 = jnp.einsum("jot,jbt->job", act, dzeta_cols, preferred_element_type=f32)
    dact = jnp.einsum("jbt,job->jot", dzeta_cols, first_down, preferred_element_type=f32)
    dpre = (dact * gelu_deriv(pre.astype(f32))).astype(bf16)
    grad_u2 = jnp.einsum("jbt,jot->jbo", upper_cols, dpre, preferred_element_type=f32)
    dupper = jnp.einsum("jot,jbo->jbt", dpre, second_up, preferred_element_type=f32).astype(bf16)
    return (grad_d1, grad_u2, dupper)


def shards(tokens, first_up, second_up, first_down, second_down, out_grad):
    f32 = jnp.float32
    bf16 = jnp.bfloat16
    tok_rows = tokens.shape[0]
    local_blocks = first_up.shape[0]
    blk_width = first_up.shape[1]
    xblk = tokens.reshape(tok_rows, local_blocks, blk_width)
    eblk = out_grad.reshape(tok_rows, local_blocks, blk_width)
    upper = jnp.einsum("tbi,bij->jbt", xblk, first_up, preferred_element_type=f32).astype(bf16)
    upper_cols = lax.all_to_all(upper, "tensor", split_axis=0, concat_axis=1, tiled=True)
    pre, act, zeta = middle_work(upper_cols, second_up, first_down)
    zeta_rows = lax.all_to_all(zeta, "tensor", split_axis=1, concat_axis=0, tiled=True)
    grad_d2 = jnp.einsum("jbt,tbk->bjk", zeta_rows, eblk, preferred_element_type=f32)
    dzeta = jnp.einsum("tbk,bjk->jbt", eblk, second_down, preferred_element_type=f32).astype(bf16)
    dzeta_cols = lax.all_to_all(dzeta, "tensor", split_axis=0, concat_axis=1, tiled=True)
    grad_d1, grad_u2, dupper = column_backward(
        dzeta_cols, act, pre, upper_cols, second_up, first_down
    )
    dupper_rows = lax.all_to_all(dupper, "tensor", split_axis=1, concat_axis=0, tiled=True)
    output = jnp.einsum("jbt,bjk->tbk", zeta_rows, second_down, preferred_element_type=f32).astype(
        bf16
    )
    output = output.reshape(tok_rows, local_blocks * blk_width)
    grad_u1 = jnp.einsum("tbi,jbt->bij", xblk, dupper_rows, preferred_element_type=f32)
    grad_u1, grad_u2, grad_d1, grad_d2 = lax.psum((grad_u1, grad_u2, grad_d1, grad_d2), "dp")
    tokens_grad = jnp.einsum(
        "jbt,bij->tbi", dupper_rows, first_up, preferred_element_type=f32
    ).astype(bf16)
    tokens_grad = tokens_grad.reshape(tok_rows, local_blocks * blk_width)
    return (output, tokens_grad, grad_u1, grad_u2, grad_d1, grad_d2)


def solution(mesh):
    placed = (
        P("dp", "tensor"),
        P("tensor", None, None),
        P("tensor", None, None),
        P("tensor", None, None),
        P("tensor", None, None),
        P("dp", "tensor"),
    )
    return jax.shard_map(
        shards,
        mesh=mesh,
        in_specs=placed,
        out_specs=(
            P("dp", "tensor"),
            P("dp", "tensor"),
            P("tensor", None, None),
            P("tensor", None, None),
            P("tensor", None, None),
            P("tensor", None, None),
        ),
        check_vma=False,
    )
```

profile of v0, /device:TPU:102, one launch (start us, length us, event | category | flops | bytes accessed | tf_op | source)
XLA Modules:
  0.0 323.2 jit_solution(2137689660007310916)
XLA Ops:
  7.2 0.0 copy-start
  7.2 0.0 copy-start.3
  7.2 0.9 copy-done
  8.1 1.0 fusion.12
  9.1 0.5 broadcast.19
  9.6 0.8 reduce.2
  10.4 0.8 reshape.62
  11.2 14.9 %all-to-all-start = ((bf16[64,2,1024]{2,1,0:T(2,128)(2,1)}), bf16[64,2,1024]{2,1,0:T(2,128)(2,1)S(1)}, u32[]{:S(2)}, u32[]{:S(2)}) async-start(bf16[64,2,1024]{2,1,0:T(2,128)(2,1)} %reshape.62), calls=%async_computation | async-start | bytes 524288 | tf_op jit(solution)/shard_map/all_to_all | solution.py:46
  26.2 0.2 fusion.13
  26.4 0.8 reduce.3
  27.2 0.8 reshape.64
  28.0 13.2 %all-to-all-done = bf16[64,2,1024]{2,1,0:T(2,128)(2,1)S(1)} async-done(((bf16[64,2,1024]{2,1,0:T(2,128)(2,1)}), bf16[64,2,1024]{2,1,0:T(2,128)(2,1)S(1)}, u32[]{:S(2)}, u32[]{:S(2)}) %all-to-all-start) | async-done | bytes 262176 | tf_op jit(solution)/shard_map/all_to_all | solution.py:46
  41.2 11.1 %all-to-all-start.2 = ((bf16[64,2,1024]{2,1,0:T(2,128)(2,1)}), bf16[64,2,1024]{2,1,0:T(2,128)(2,1)S(1)}, u32[]{:S(2)}, u32[]{:S(2)}) async-start(bf16[64,2,1024]{2,1,0:T(2,128)(2,1)} %reshape.64), calls=%async_computation.2 | async-start | bytes 524288 | tf_op jit(solution)/shard_map/all_to_all | solution.py:51
  52.3 0.0 copy-start.4
  52.3 0.2 reshape.63
  52.6 1.5 reduce
  54.1 0.8 all_to_all.49
  54.9 12.5 %all-to-all-done.2 = bf16[64,2,1024]{2,1,0:T(2,128)(2,1)S(1)} async-done(((bf16[64,2,1024]{2,1,0:T(2,128)(2,1)}), bf16[64,2,1024]{2,1,0:T(2,128)(2,1)S(1)}, u32[]{:S(2)}, u32[]{:S(2)}) %all-to-all-start.2) | async-done | bytes 262176 | tf_op jit(solution)/shard_map/all_to_all | solution.py:51
  67.4 0.2 reshape.65
  67.6 1.5 reduce.1
  69.1 0.8 all_to_all.56
  69.9 0.0 copy-done.4
  70.0 1.5 fusion.8
  71.5 0.8 fusion.5
  72.4 1.0 copy-done.1
  73.3 0.4 fusion.11
  73.8 1.0 copy.44
  74.7 11.3 %all-to-all-start.3 = ((bf16[2,64,1024]{2,0,1:T(2,128)(2,1)}), bf16[2,64,1024]{2,0,1:T(2,128)(2,1)}, u32[]{:S(2)}, u32[]{:S(2)}) async-start(bf16[2,64,1024]{2,0,1:T(2,128)(2,1)} %copy.44), calls=%async_computation.3 | async-start | bytes 524288 | tf_op jit(solution)/shard_map/all_to_all | solution.py:55
  86.1 1.3 fusion.10
  87.3 1.0 copy.40
  88.3 12.7 %all-to-all-done.3 = bf16[2,64,1024]{2,0,1:T(2,128)(2,1)} async-done(((bf16[2,64,1024]{2,0,1:T(2,128)(2,1)}), bf16[2,64,1024]{2,0,1:T(2,128)(2,1)}, u32[]{:S(2)}, u32[]{:S(2)}) %all-to-all-start.3) | async-done | bytes 262176 | tf_op jit(solution)/shard_map/all_to_all | solution.py:55
  101.0 11.3 %all-to-all-start.1 = ((bf16[2,64,1024]{2,0,1:T(2,128)(2,1)}), bf16[2,64,1024]{2,0,1:T(2,128)(2,1)}, u32[]{:S(2)}, u32[]{:S(2)}) async-start(bf16[2,64,1024]{2,0,1:T(2,128)(2,1)} %copy.40), calls=%async_computation.1 | async-start | bytes 524288 | tf_op jit(solution)/shard_map/all_to_all | solution.py:48
  112.3 0.0 all-reduce.3.cloned.1.call-start
  112.4 2.3 fusion.17
  114.7 2.0 fusion.14
  116.6 1.1 reshape.59
  117.7 0.8 convolution_bitcast_fusion.1
  118.5 8.8 %all-to-all-done.1 = bf16[2,64,1024]{2,0,1:T(2,128)(2,1)} async-done(((bf16[2,64,1024]{2,0,1:T(2,128)(2,1)}), bf16[2,64,1024]{2,0,1:T(2,128)(2,1)}, u32[]{:S(2)}, u32[]{:S(2)}) %all-to-all-start.1) | async-done | bytes 262176 | tf_op jit(solution)/shard_map/all_to_all | solution.py:48
  127.3 1.0 reshape.57
  128.4 1.8 convolution_bitcast_fusion
  130.2 0.0 all-reduce.3.cloned.1.call-update
  130.2 1.0 convolution_convert_fusion.1
  131.2 1.0 convolution_convert_fusion.3
  132.1 178.1 %all-reduce.3.cloned.1.call-done = (f32[1,128,128]{1,2,0:T(8,128)}, f32[2,64,256]{2,1,0:T(8,128)}, f32[2,256,64]{1,2,0:T(8,128)}, f32[1,128,128]{2,1,0:T(8,128)}) async-done(((f32[1,128,128]{1,2,0:T(8,128)}, f32[2,64,256]{2,1,0:T(8,128)}, f32[2,256,64]{1,2,0:T(8,128)}, f32[1,128,128]{2,1,0:T(8,128)}), (f32[1,128,128]{1,2,0:T(8,128)}, f32[2,64,256]{2,1,0:T(8,128)}, f32[2,256,64]{1,2,0:T(8,128)}, ...) | async-done | bytes 393232 | tf_op jit(solution)/shard_map/psum | solution.py:61
  310.2 1.6 copy.47
  311.8 1.6 copy.80
  313.4 1.6 copy.81
  314.9 1.5 copy.82
  (10 shorter events, 0.0 us)
Async XLA Ops:
  7.2 1.0 copy-start
  7.2 19.0 %copy-start.6 = (bf16[1,128,128]{2,1,0:T(8,128)(2,1)S(1)}, bf16[1,128,128]{2,1,0:T(8,128)(2,1)}, u32[]{:S(2)}) copy-start(bf16[1,128,128]{2,1,0:T(8,128)(2,1)} %param.10) | copy-start | bytes 98308
  7.2 19.0 %copy-start.3 = (bf16[1024,128]{1,0:T(8,128)(2,1)S(1)}, bf16[1024,128]{1,0:T(8,128)(2,1)}, u32[]{:S(2)}) copy-start(bf16[1024,128]{1,0:T(8,128)(2,1)} %param.11) | copy-start | bytes 786436
  11.2 30.0 %all-to-all-start = ((bf16[64,2,1024]{2,1,0:T(2,128)(2,1)}), bf16[64,2,1024]{2,1,0:T(2,128)(2,1)S(1)}, u32[]{:S(2)}, u32[]{:S(2)}) async-start(bf16[64,2,1024]{2,1,0:T(2,128)(2,1)} %reshape.62), calls=%async_computation | async-start | bytes 524288 | tf_op jit(solution)/shard_map/all_to_all | solution.py:46
  41.2 26.2 %all-to-all-start.2 = ((bf16[64,2,1024]{2,1,0:T(2,128)(2,1)}), bf16[64,2,1024]{2,1,0:T(2,128)(2,1)S(1)}, u32[]{:S(2)}, u32[]{:S(2)}) async-start(bf16[64,2,1024]{2,1,0:T(2,128)(2,1)} %reshape.64), calls=%async_computation.2 | async-start | bytes 524288 | tf_op jit(solution)/shard_map/all_to_all | solution.py:51
  52.3 17.6 %copy-start.4 = (bf16[2,64,256]{2,1,0:T(8,128)(2,1)S(1)}, bf16[2,64,256]{2,1,0:T(8,128)(2,1)}, u32[]{:S(2)}) copy-start(bf16[2,64,256]{2,1,0:T(8,128)(2,1)} %param.8) | copy-start | bytes 196612
  69.9 1.6 copy-start.2
  70.0 1.6 copy-start.7
  72.4 1.0 copy-start.1
  74.7 26.3 %all-to-all-start.3 = ((bf16[2,64,1024]{2,0,1:T(2,128)(2,1)}), bf16[2,64,1024]{2,0,1:T(2,128)(2,1)}, u32[]{:S(2)}, u32[]{:S(2)}) async-start(bf16[2,64,1024]{2,0,1:T(2,128)(2,1)} %copy.44), calls=%async_computation.3 | async-start | bytes 524288 | tf_op jit(solution)/shard_map/all_to_all | solution.py:55
  101.0 26.3 %all-to-all-start.1 = ((bf16[2,64,1024]{2,0,1:T(2,128)(2,1)}), bf16[2,64,1024]{2,0,1:T(2,128)(2,1)}, u32[]{:S(2)}, u32[]{:S(2)}) async-start(bf16[2,64,1024]{2,0,1:T(2,128)(2,1)} %copy.40), calls=%async_computation.1 | async-start | bytes 524288 | tf_op jit(solution)/shard_map/all_to_all | solution.py:48
  112.3 197.9 %all-reduce.3.cloned.1.call-start = ((), (), s32[]{:S(2)}) async-start(), calls=%async_computation.4 | async-start | bytes 786432 | tf_op jit(solution)/shard_map/psum | solution.py:61
  116.6 13.6 %copy-start.5 = (bf16[1,128,128]{2,1,0:T(8,128)(2,1)S(1)}, bf16[1,128,128]{2,1,0:T(8,128)(2,1)}, u32[]{:S(2)}) copy-start(bf16[1,128,128]{2,1,0:T(8,128)(2,1)} %param.7) | copy-start | bytes 98308
Sparse Core Ops, SparseCore 0:
  130.3 179.8 all-reduce.2
where the time goes:
time: 324 us; the launch traced here: 323 us
  waiting for transfers between devices  225 us (69%)
  starting transfers between devices  48.7 us (15%)
  local copies, waits for them, and re-layouts  16.3 us (5%)
  between operations  14.2 us (4%)
  matrix products  14.1 us (4%)
  other arithmetic  4.59 us (1%)
    psum x1, waiting for transfers between devices, shards(): lax.psum((grad_u1, grad_u2, grad_d1, grad_d2), 'dp')  178 us
    all_to_all x1, starting transfers between devices, shards(): lax.all_to_all(upper, 'tensor', split_axis=0, concat_axis=1, tiled=True)  14.9 us
    all_to_all x1, waiting for transfers between devices, shards(): lax.all_to_all(upper, 'tensor', split_axis=0, concat_axis=1, tiled=True)  13.2 us
    all_to_all x1, waiting for transfers between devices, shards(): lax.all_to_all(dupper, 'tensor', split_axis=1, concat_axis=0, tiled=True)  12.7 us
    all_to_all x1, waiting for transfers between devices, shards(): lax.all_to_all(dzeta, 'tensor', split_axis=0, concat_axis=1, tiled=True)  12.5 us
    all_to_all x1, starting transfers between devices, shards(): lax.all_to_all(dupper, 'tensor', split_axis=1, concat_axis=0, tiled=True)  11.3 us
    all_to_all x1, starting transfers between devices, shards(): lax.all_to_all(zeta, 'tensor', split_axis=1, concat_axis=0, tiled=True)  11.3 us
    all_to_all x1, starting transfers between devices, shards(): lax.all_to_all(dzeta, 'tensor', split_axis=0, concat_axis=1, tiled=True)  11.1 us
  transfers between devices with their start and end apart: 5, of which 5 were waited for; matrix products, arithmetic and copies ran while one was open for 4% of the time, Pallas kernels for 0%

commit v1 on v0

--- a/solution.py
+++ b/solution.py
@@ -48,7 +48,12 @@
     zeta_rows = lax.all_to_all(zeta, "tensor", split_axis=1, concat_axis=0, tiled=True)
     grad_d2 = jnp.einsum("jbt,tbk->bjk", zeta_rows, eblk, preferred_element_type=f32)
     dzeta = jnp.einsum("tbk,bjk->jbt", eblk, second_down, preferred_element_type=f32).astype(bf16)
-    dzeta_cols = lax.all_to_all(dzeta, "tensor", split_axis=0, concat_axis=1, tiled=True)
+    dzeta_cols = jnp.concatenate(
+        lax.all_to_all(
+            jnp.stack(jnp.split(dzeta, lax.axis_size("tensor"), axis=0)), "tensor", 0, 0
+        ),
+        axis=1,
+    )
     grad_d1, grad_u2, dupper = column_backward(
         dzeta_cols, act, pre, upper_cols, second_up, first_down
     )

time: 324 us -> 347 us (1.071)
  local copies, waits for them, and re-layouts: 16.3 us -> 52.8 us
  waiting for transfers between devices: 225 us -> 211 us
    unnamed x24 -> x81, local copies, waits for them, and re-layouts: 10.2 us -> 46.8 us
    all_to_all x1, waiting for transfers between devices: 13.2 us -> 0.01 us  [shards(): lax.all_to_all(upper, 'tensor', split_axis=0, concat_axis=1, tiled=True)]
  transfers between devices with their start and end apart: 5 -> 5, of which waited for: 5 -> 4; matrix products, arithmetic and copies ran while one was open for 4% -> 15% of each run, Pallas kernels for 0% -> 0%
where the time goes in v1:
time: 347 us; the launch traced here: 346 us
  waiting for transfers between devices  211 us (61%)
  local copies, waits for them, and re-layouts  52.8 us (15%)
  starting transfers between devices  50.9 us (15%)
  matrix products  15 us (4%)
  between operations  14.2 us (4%)
    psum x1, waiting for transfers between devices, shards(): lax.psum((grad_u1, grad_u2, grad_d1, grad_d2), 'dp')  178 us
    unnamed x81, local copies, waits for them, and re-layouts  46.8 us
    all_to_all x1, starting transfers between devices, shards(): lax.all_to_all(upper, 'tensor', split_axis=0, concat_axis=1, tiled=True)  15 us
    all_to_all x1, starting transfers between devices, shards(): lax.all_to_all(jnp.stack(jnp.split(dzeta, lax.axis_size('tensor'), axis=0...  13.3 us
    all_to_all x1, waiting for transfers between devices, shards(): lax.all_to_all(dupper, 'tensor', split_axis=1, concat_axis=0, tiled=True)  12.7 us
    all_to_all x1, starting transfers between devices, shards(): lax.all_to_all(zeta, 'tensor', split_axis=1, concat_axis=0, tiled=True)  11.3 us
    all_to_all x1, starting transfers between devices, shards(): lax.all_to_all(dupper, 'tensor', split_axis=1, concat_axis=0, tiled=True)  11.3 us
    all_to_all x1, waiting for transfers between devices, shards(): lax.all_to_all(jnp.stack(jnp.split(dzeta, lax.axis_size('tensor'), axis=0...  10.9 us
  transfers between devices with their start and end apart: 5, of which 4 were waited for; matrix products, arithmetic and copies ran while one was open for 15% of the time, Pallas kernels for 0%

profile of v1, /device:TPU:102, one launch (start us, length us, event | category | flops | bytes accessed | tf_op | source)
XLA Modules:
  0.0 346.1 jit_solution(13217377398322833098)
XLA Ops:
  7.2 0.9 copy-done
  8.1 1.0 fusion.12
  9.6 0.8 reduce.1
  10.4 0.8 reshape.197
  11.2 15.0 %all-to-all-start = ((bf16[64,2,1024]{2,1,0:T(2,128)(2,1)}), bf16[64,2,1024]{2,1,0:T(2,128)(2,1)S(1)}, u32[]{:S(2)}, u32[]{:S(2)}) async-start(bf16[64,2,1024]{2,1,0:T(2,128)(2,1)} %reshape.197), calls=%async_computation | async-start | bytes 524288 | tf_op jit(solution)/shard_map/all_to_all | solution.py:46
  27.7 0.6 constant_dynamic-update-slice_fusion.61
  28.3 0.6 constant_dynamic-update-slice_fusion.60
  29.5 0.6 constant_dynamic-update-slice_fusion.58
  32.5 0.6 constant_dynamic-update-slice_fusion.53
  34.3 0.6 constant_dynamic-update-slice_fusion.50
  37.3 0.6 constant_dynamic-update-slice_fusion.45
  39.1 0.6 constant_dynamic-update-slice_fusion.42
  42.1 0.6 constant_dynamic-update-slice_fusion.37
  45.1 0.6 constant_dynamic-update-slice_fusion.32
  46.9 0.6 constant_dynamic-update-slice_fusion.29
  49.9 0.6 constant_dynamic-update-slice_fusion.24
  51.7 0.6 constant_dynamic-update-slice_fusion.21
  54.7 0.6 constant_dynamic-update-slice_fusion.16
  55.9 0.6 constant_dynamic-update-slice_fusion.14
  56.5 0.6 constant_dynamic-update-slice_fusion.13
  59.5 0.6 constant_dynamic-update-slice_fusion.8
  64.9 13.3 %all-to-all-start.2 = ((bf16[64,2,1,1024]{3,1,2,0:T(2,128)(2,1)}), bf16[64,2,1,1024]{3,1,2,0:T(2,128)(2,1)}, u32[]{:S(2)}, u32[]{:S(2)}) async-start(bf16[64,2,1,1024]{3,1,2,0:T(2,128)(2,1)} %constant_dynamic-update-slice_fusion), calls=%async_computation.2 | async-start | bytes 524288 | tf_op jit(solution)/shard_map/all_to_all | solution.py:52
  78.4 1.5 reduce
  79.9 0.8 all_to_all.39
  80.7 1.5 fusion.8
  82.2 10.9 %all-to-all-done.2 = bf16[64,2,1,1024]{3,1,2,0:T(2,128)(2,1)} async-done(((bf16[64,2,1,1024]{3,1,2,0:T(2,128)(2,1)}), bf16[64,2,1,1024]{3,1,2,0:T(2,128)(2,1)}, u32[]{:S(2)}, u32[]{:S(2)}) %all-to-all-start.2) | async-done | bytes 262176 | tf_op jit(solution)/shard_map/all_to_all | solution.py:52
  93.1 1.8 fusion.5
  94.9 1.0 copy-done.1
  96.3 1.0 copy.46
  97.3 11.3 %all-to-all-start.3 = ((bf16[2,64,1024]{2,0,1:T(2,128)(2,1)}), bf16[2,64,1024]{2,0,1:T(2,128)(2,1)}, u32[]{:S(2)}, u32[]{:S(2)}) async-start(bf16[2,64,1024]{2,0,1:T(2,128)(2,1)} %copy.46), calls=%async_computation.3 | async-start | bytes 524288 | tf_op jit(solution)/shard_map/all_to_all | solution.py:60
  108.6 1.3 fusion.10
  109.9 1.0 copy.43
  110.9 12.7 %all-to-all-done.3 = bf16[2,64,1024]{2,0,1:T(2,128)(2,1)} async-done(((bf16[2,64,1024]{2,0,1:T(2,128)(2,1)}), bf16[2,64,1024]{2,0,1:T(2,128)(2,1)}, u32[]{:S(2)}, u32[]{:S(2)}) %all-to-all-start.3) | async-done | bytes 262176 | tf_op jit(solution)/shard_map/all_to_all | solution.py:60
  123.6 11.3 %all-to-all-start.1 = ((bf16[2,64,1024]{2,0,1:T(2,128)(2,1)}), bf16[2,64,1024]{2,0,1:T(2,128)(2,1)}, u32[]{:S(2)}, u32[]{:S(2)}) async-start(bf16[2,64,1024]{2,0,1:T(2,128)(2,1)} %copy.43), calls=%async_computation.1 | async-start | bytes 524288 | tf_op jit(solution)/shard_map/all_to_all | solution.py:48
  134.9 2.3 fusion.13
  137.2 2.0 fusion.16
  139.2 1.1 reshape.195
  140.2 0.8 convolution_bitcast_fusion.1
  141.1 8.8 %all-to-all-done.1 = bf16[2,64,1024]{2,0,1:T(2,128)(2,1)} async-done(((bf16[2,64,1024]{2,0,1:T(2,128)(2,1)}), bf16[2,64,1024]{2,0,1:T(2,128)(2,1)}, u32[]{:S(2)}, u32[]{:S(2)}) %all-to-all-start.1) | async-done | bytes 262176 | tf_op jit(solution)/shard_map/all_to_all | solution.py:48
  149.9 1.0 reshape.191
  150.9 1.8 convolution_bitcast_fusion
  152.8 1.0 convolution_convert_fusion.1
  153.7 1.0 convolution_convert_fusion.3
  154.7 178.4 %all-reduce.3.cloned.1.call-done = (f32[1,128,128]{1,2,0:T(8,128)}, f32[2,64,256]{2,1,0:T(8,128)}, f32[2,256,64]{1,2,0:T(8,128)}, f32[1,128,128]{2,1,0:T(8,128)}) async-done(((f32[1,128,128]{1,2,0:T(8,128)}, f32[2,64,256]{2,1,0:T(8,128)}, f32[2,256,64]{1,2,0:T(8,128)}, f32[1,128,128]{2,1,0:T(8,128)}), (f32[1,128,128]{1,2,0:T(8,128)}, f32[2,64,256]{2,1,0:T(8,128)}, f32[2,256,64]{1,2,0:T(8,128)}, ...) | async-done | bytes 393232 | tf_op jit(solution)/shard_map/psum | solution.py:66
  333.1 1.6 copy.50
  334.6 1.6 copy.139
  336.2 1.6 copy.140
  337.8 1.5 copy.141
  (65 shorter events, 30.2 us)
Async XLA Ops:
  7.2 1.0 copy-start
  7.2 19.1 %copy-start.5 = (bf16[1,128,128]{2,1,0:T(8,128)(2,1)S(1)}, bf16[1,128,128]{2,1,0:T(8,128)(2,1)}, u32[]{:S(2)}) copy-start(bf16[1,128,128]{2,1,0:T(8,128)(2,1)} %param.10) | copy-start | bytes 98308
  7.2 19.1 %copy-start.2 = (bf16[1024,128]{1,0:T(8,128)(2,1)S(1)}, bf16[1024,128]{1,0:T(8,128)(2,1)}, u32[]{:S(2)}) copy-start(bf16[1024,128]{1,0:T(8,128)(2,1)} %param.11) | copy-start | bytes 786436
  11.2 69.5 %copy-start.3 = (bf16[2,64,256]{2,1,0:T(8,128)(2,1)S(1)}, bf16[2,64,256]{2,1,0:T(8,128)(2,1)}, u32[]{:S(2)}) copy-start(bf16[2,64,256]{2,1,0:T(8,128)(2,1)} %param.8) | copy-start | bytes 196612
  11.2 53.6 %all-to-all-start = ((bf16[64,2,1024]{2,1,0:T(2,128)(2,1)}), bf16[64,2,1024]{2,1,0:T(2,128)(2,1)S(1)}, u32[]{:S(2)}, u32[]{:S(2)}) async-start(bf16[64,2,1024]{2,1,0:T(2,128)(2,1)} %reshape.197), calls=%async_computation | async-start | bytes 524288 | tf_op jit(solution)/shard_map/all_to_all | solution.py:46
  64.9 28.2 %all-to-all-start.2 = ((bf16[64,2,1,1024]{3,1,2,0:T(2,128)(2,1)}), bf16[64,2,1,1024]{3,1,2,0:T(2,128)(2,1)}, u32[]{:S(2)}, u32[]{:S(2)}) async-start(bf16[64,2,1,1024]{3,1,2,0:T(2,128)(2,1)} %constant_dynamic-update-slice_fusion), calls=%async_computation.2 | async-start | bytes 524288 | tf_op jit(solution)/shard_map/all_to_all | solution.py:52
  94.9 1.0 copy-start.1
  97.3 26.3 %all-to-all-start.3 = ((bf16[2,64,1024]{2,0,1:T(2,128)(2,1)}), bf16[2,64,1024]{2,0,1:T(2,128)(2,1)}, u32[]{:S(2)}, u32[]{:S(2)}) async-start(bf16[2,64,1024]{2,0,1:T(2,128)(2,1)} %copy.46), calls=%async_computation.3 | async-start | bytes 524288 | tf_op jit(solution)/shard_map/all_to_all | solution.py:60
  123.6 26.3 %all-to-all-start.1 = ((bf16[2,64,1024]{2,0,1:T(2,128)(2,1)}), bf16[2,64,1024]{2,0,1:T(2,128)(2,1)}, u32[]{:S(2)}, u32[]{:S(2)}) async-start(bf16[2,64,1024]{2,0,1:T(2,128)(2,1)} %copy.43), calls=%async_computation.1 | async-start | bytes 524288 | tf_op jit(solution)/shard_map/all_to_all | solution.py:48
  134.9 198.2 %all-reduce.3.cloned.1.call-start = ((), (), s32[]{:S(2)}) async-start(), calls=%async_computation.4 | async-start | bytes 786432 | tf_op jit(solution)/shard_map/psum | solution.py:66
  139.2 13.6 %copy-start.4 = (bf16[1,128,128]{2,1,0:T(8,128)(2,1)S(1)}, bf16[1,128,128]{2,1,0:T(8,128)(2,1)}, u32[]{:S(2)}) copy-start(bf16[1,128,128]{2,1,0:T(8,128)(2,1)} %param.7) | copy-start | bytes 98308
Sparse Core Ops, SparseCore 0:
  152.9 180.1 all-reduce.2
